TPU v7x, 512 devices: a whole 4x8x8 slice. The times are simulated.
512 devices in a mesh: row: 64 (over x, z, core), col: 8 (over y).
Axes of the slice: x: 4, y: 8, z: 8, core: 2. Of those that a mesh axis runs over, the one named last changes fastest.
Arguments:
- trailing: float32 [32768, 8192], P('row', 'col'), may hold values from -6 to 6
- reflectors: float32 [32768, 256], P('row', 'col'), may hold values from -0.25 to 0.25
- leaf_factor: float32 [16384, 256], P('row', 'col'), may hold values from -0.5 to 0.5
- node_reflect: float32 [6, 16384, 256], P(None, 'row', 'col'), may hold values from -0.375 to 0.375
- node_factor: float32 [6, 16384, 256], P(None, 'row', 'col'), may hold values from -0.5 to 0.5
Outputs:
- updated: float32 [32768, 8192], P('row', 'col')
All inputs are finite; a program needn't handle non-finite values.
Results may differ from a plain program's by a relative error of at most 0.00014.
Values sent between devices are 32-bit elements; how exact they have to be, the bound alone decides.
A program may use at most 64 MiB of HBM per device.

v0:
```python
import jax
import jax.numpy as jnp
from jax import lax
from jax.sharding import PartitionSpec as P

B = 256
highest = lax.Precision.HIGHEST


def turned_gather(arrays, axis, dims):
    turned = [jnp.moveaxis(a, dim, 0) for a, dim in zip(arrays, dims)]
    both = jnp.concatenate([t.reshape(len(t), -1) for t in turned], axis=1)
    whole, at, done = (lax.all_gather(both, axis, axis=0, tiled=True), 0, [])
    for t, dim in zip(turned, dims):
        section = whole[:, at : at + t[0].size].reshape(-1, *t.shape[1:])
        done.append(jnp.moveaxis(section, 0, dim))
        at += t[0].size
    return tuple(done)


def swapped(value, axis, apart):
    mask = 2**apart
    pairs = [(source, source ^ mask) for source in range(lax.axis_size(axis))]
    return lax.ppermute(value, axis, pairs)


def triangle(factor):
    return jnp.triu(factor) + 0.5 * jnp.eye(factor.shape[-1], dtype=factor.dtype)


def combine(upper_rows, partner_rows, other_piece, node_y, node_full, clear):
    chosen_y = jnp.where(clear, other_piece, node_y)
    chosen_tri = triangle(jnp.where(clear, node_full, other_piece))
    leader_rows = jnp.where(clear, upper_rows, partner_rows)
    follower_rows = jnp.where(clear, partner_rows, upper_rows)
    summed = leader_rows + jnp.einsum("kb,kc->bc", chosen_y, follower_rows, precision=highest)
    coupling = jnp.einsum("kb,kc->bc", chosen_tri, summed, precision=highest)
    lowered = upper_rows - jnp.einsum("bk,kc->bc", chosen_y, coupling, precision=highest)
    return jnp.where(clear, upper_rows - coupling, lowered)


def per_device(trailing, reflectors, leaf_factor, node_reflect, node_factor):
    vectors, leaf_full, node_y_all, node_f_all = turned_gather(
        (reflectors, leaf_factor, node_reflect, node_factor), "col", (1, 1, 2, 2)
    )
    leaf_tri = triangle(leaf_full)
    inner = jnp.einsum("rb,rc->bc", vectors, trailing, precision=highest)
    scaled = jnp.einsum("kb,kc->bc", leaf_tri, inner, precision=highest)
    leafed = trailing - jnp.einsum("rb,bc->rc", vectors, scaled, precision=highest)
    upper_rows = leafed[:B]
    remainder = leafed[B:]
    position = lax.axis_index("row")
    levels = lax.axis_size("row").bit_length() - 1
    clears = []
    pieces = []
    for section in range(levels):
        clear = position // (1 << section) % 2 == 0
        clears.append(clear)
        pieces.append(jnp.where(clear, node_f_all[section], node_y_all[section]))
    for section in range(levels):
        partner_rows, other_piece = swapped((upper_rows, pieces[section]), "row", section)
        upper_rows = combine(
            upper_rows,
            partner_rows,
            other_piece,
            node_y_all[section],
            node_f_all[section],
            clears[section],
        )
    return jnp.concatenate([upper_rows, remainder], axis=0)


def solution(mesh):
    in_specs = (
        P("row", "col"),
        P("row", "col"),
        P("row", "col"),
        P(None, "row", "col"),
        P(None, "row", "col"),
    )
    out_specs = P("row", "col")
    return jax.shard_map(
        per_device, mesh=mesh, in_specs=in_specs, out_specs=out_specs, check_vma=False
    )
```

profile of v0, /device:TPU:2, one launch (start us, length us, event | category | flops | bytes accessed | tf_op | source)
XLA Modules:
  0.0 353.9 jit_solution(16999531259912984661)
XLA Ops:
  6.5 0.0 all-gather.2.cloned.1.call-start
  6.5 1.1 copy.14
  7.6 0.9 copy.15
  8.6 1.7 pad_maximum_fusion.1
  10.3 0.0 all-gather.2.cloned.1.call-update
  10.4 59.3 %all-gather.2.cloned.1.call-done = f32[256,3840]{1,0:T(8,128)} async-done(((f32[32,3840]{1,0:T(8,128)}), f32[256,3840]{1,0:T(8,128)}) %all-gather.2.cloned.1.call-update) | async-done | bytes 3932176 | tf_op jit(solution)/shard_map/all_gather | solution.py:13
  69.7 0.0 copy-done.2
  69.7 3.1 fusion.43
  72.8 0.0 copy-start.3
  72.8 2.1 fusion.45
  74.9 0.0 copy-done.4
  74.9 0.0 copy-done.3
  75.0 1.9 convolution_subtract_fusion
  76.9 1.2 fusion.140
  78.1 1.9 collective-permute-start.1
  80.0 2.1 fusion.139
  82.1 3.0 copy.12
  85.2 3.0 copy.13
  88.2 3.0 copy.10
  91.2 3.0 copy.11
  94.3 2.1 fusion.70
  96.4 2.5 collective-permute-start
  99.0 1.1 collective-permute-done
  100.1 0.0 collective-permute-done.1
  100.1 2.3 fusion.27
  102.4 0.0 copy-done.1
  102.4 1.2 fusion.25
  103.6 1.2 subtract_select_fusion.5
  104.8 3.6 %collective-permute-start.3 = (f32[256,1024]{1,0:T(8,128)S(1)}, f32[256,1024]{1,0:T(8,128)S(1)}, u32[]{:S(2)}, u32[]{:S(2)}) collective-permute-start(f32[256,1024]{1,0:T(8,128)S(1)} %subtract_select_fusion.5), channel_id=1, source_target_pairs={{0,16},{8,24},{16,0},{24,8},{32,48},{40,56},{48,32},{56,40},{64,80... | collective-permute-start | bytes 3145736 | tf_op jit(solution)/shard_map/ppermute | solution.py:24
  108.3 2.5 collective-permute-start.2
  110.8 26.9 %collective-permute-done.2 = f32[256,256]{0,1:T(8,128)S(1)} collective-permute-done((f32[256,256]{0,1:T(8,128)S(1)}, f32[256,256]{0,1:T(8,128)S(1)}, u32[]{:S(2)}, u32[]{:S(2)}) %collective-permute-start.2) | collective-permute-done | bytes 262176 | tf_op jit(solution)/shard_map/ppermute | solution.py:24
  137.7 0.0 collective-permute-done.3
  137.7 1.1 fusion.22
  138.8 1.2 fusion.20
  140.0 1.2 subtract_select_fusion.4
  141.2 4.6 %collective-permute-start.5 = (f32[256,1024]{1,0:T(8,128)S(1)}, f32[256,1024]{1,0:T(8,128)S(1)}, u32[]{:S(2)}, u32[]{:S(2)}) collective-permute-start(f32[256,1024]{1,0:T(8,128)S(1)} %subtract_select_fusion.4), channel_id=1, source_target_pairs={{0,32},{8,40},{16,48},{24,56},{32,0},{40,8},{48,16},{56,24},{64,96... | collective-permute-start | bytes 3145736 | tf_op jit(solution)/shard_map/ppermute | solution.py:24
  145.8 2.1 collective-permute-start.4
  147.9 54.4 %collective-permute-done.4 = f32[256,256]{0,1:T(8,128)S(1)} collective-permute-done((f32[256,256]{0,1:T(8,128)S(1)}, f32[256,256]{0,1:T(8,128)S(1)}, u32[]{:S(2)}, u32[]{:S(2)}) %collective-permute-start.4) | collective-permute-done | bytes 262176 | tf_op jit(solution)/shard_map/ppermute | solution.py:24
  202.3 0.0 collective-permute-done.5
  202.3 1.1 fusion.17
  203.4 1.2 fusion.15
  204.6 1.2 subtract_select_fusion.3
  205.8 7.9 %collective-permute-start.7 = (f32[256,1024]{1,0:T(8,128)S(1)}, f32[256,1024]{1,0:T(8,128)S(1)}, u32[]{:S(2)}, u32[]{:S(2)}) collective-permute-start(f32[256,1024]{1,0:T(8,128)S(1)} %subtract_select_fusion.3), channel_id=1, source_target_pairs={{0,64},{8,72},{16,80},{24,88},{32,96},{40,104},{48,112},{56,120},{... | collective-permute-start | bytes 3145736 | tf_op jit(solution)/shard_map/ppermute | solution.py:24
  213.7 1.9 collective-permute-start.6
  215.6 55.4 %collective-permute-done.6 = f32[256,256]{0,1:T(8,128)S(1)} collective-permute-done((f32[256,256]{0,1:T(8,128)S(1)}, f32[256,256]{0,1:T(8,128)S(1)}, u32[]{:S(2)}, u32[]{:S(2)}) %collective-permute-start.6) | collective-permute-done | bytes 262176 | tf_op jit(solution)/shard_map/ppermute | solution.py:24
  271.0 0.0 collective-permute-done.7
  271.0 1.1 fusion.12
  272.1 1.2 fusion.10
  273.3 1.2 subtract_select_fusion.2
  274.5 2.5 collective-permute-start.9
  276.9 3.6 %collective-permute-start.8 = (f32[256,256]{0,1:T(8,128)S(1)}, f32[256,256]{0,1:T(8,128)S(1)}, u32[]{:S(2)}, u32[]{:S(2)}) collective-permute-start(f32[256,256]{0,1:T(8,128)S(1)} %get-tuple-element.8), channel_id=1, source_target_pairs={{0,128},{8,136},{16,144},{24,152},{32,160},{40,168},{48,176},{56,1... | collective-permute-start | bytes 786440 | tf_op jit(solution)/shard_map/ppermute | solution.py:24
  280.5 25.7 %collective-permute-done.8 = f32[256,256]{0,1:T(8,128)S(1)} collective-permute-done((f32[256,256]{0,1:T(8,128)S(1)}, f32[256,256]{0,1:T(8,128)S(1)}, u32[]{:S(2)}, u32[]{:S(2)}) %collective-permute-start.8) | collective-permute-done | bytes 262176 | tf_op jit(solution)/shard_map/ppermute | solution.py:24
  306.2 0.0 collective-permute-done.9
  306.2 1.1 fusion.7
  307.3 1.2 fusion.5
  308.5 1.2 subtract_select_fusion.1
  309.7 4.0 %collective-permute-start.11 = (f32[256,1024]{1,0:T(8,128)S(1)}, f32[256,1024]{1,0:T(8,128)S(1)}, u32[]{:S(2)}, u32[]{:S(2)}) collective-permute-start(f32[256,1024]{1,0:T(8,128)S(1)} %subtract_select_fusion.1), channel_id=1, source_target_pairs={{0,256},{8,264},{16,272},{24,280},{32,288},{40,296},{48,304},{56,3... | collective-permute-start | bytes 3145736 | tf_op jit(solution)/shard_map/ppermute | solution.py:24
  313.7 3.4 collective-permute-start.10
  317.0 25.1 %collective-permute-done.10 = f32[256,256]{0,1:T(8,128)S(1)} collective-permute-done((f32[256,256]{0,1:T(8,128)S(1)}, f32[256,256]{0,1:T(8,128)S(1)}, u32[]{:S(2)}, u32[]{:S(2)}) %collective-permute-start.10) | collective-permute-done | bytes 262176 | tf_op jit(solution)/shard_map/ppermute | solution.py:24
  342.1 0.0 collective-permute-done.11
  342.1 1.1 fusion.2
  343.2 1.2 fusion
  344.4 1.2 subtract_select_fusion
  345.6 1.5 pad_maximum_fusion
  (6 shorter events, 0.0 us)
Async XLA Ops:
  6.5 63.1 %copy-start.2 = (f32[512,1024]{1,0:T(8,128)S(1)}, f32[512,1024]{1,0:T(8,128)}, u32[]{:S(2)}) copy-start(f32[512,1024]{1,0:T(8,128)} %param.5) | copy-start | bytes 6291460
  6.5 63.1 %all-gather.2.cloned.1.call-start = ((), (), s32[]{:S(2)}) async-start(), calls=%async_computation | async-start | bytes 4423680 | tf_op jit(solution)/shard_map/all_gather | solution.py:13
  69.7 5.3 %copy-start.4 = (f32[256,3840]{1,0:T(8,128)S(1)}, f32[256,3840]{1,0:T(8,128)}, u32[]{:S(2)}) copy-start(f32[256,3840]{1,0:T(8,128)} %all-gather.2.cloned.1.call-done) | copy-start | bytes 11796484
  72.8 2.2 copy-start.3
  78.1 22.0 %collective-permute-start.1 = (f32[256,1024]{1,0:T(8,128)}, f32[256,1024]{1,0:T(8,128)}, u32[]{:S(2)}, u32[]{:S(2)}) collective-permute-start(f32[256,1024]{1,0:T(8,128)} %get-tuple-element.13), channel_id=1, source_target_pairs={{0,8},{8,0},{16,24},{24,16},{32,40},{40,32},{48,56},{56,48},{64,72... | collective-permute-start | bytes 3145736 | tf_op jit(solution)/shard_map/ppermute | solution.py:24
  94.3 5.8 %copy-start = (f32[256,6,256]{2,0,1:T(8,128)S(1)}, f32[256,6,256]{2,0,1:T(8,128)}, u32[]{:S(2)}) copy-start(f32[256,6,256]{2,0,1:T(8,128)} %copy.13) | copy-start | bytes 4718596
  96.4 6.0 %copy-start.1 = (f32[256,6,256]{2,0,1:T(8,128)S(1)}, f32[256,6,256]{2,0,1:T(8,128)}, u32[]{:S(2)}) copy-start(f32[256,6,256]{2,0,1:T(8,128)} %copy.11) | copy-start | bytes 4718596
  96.4 3.7 %collective-permute-start = (f32[256,256]{0,1:T(8,128)S(1)}, f32[256,256]{0,1:T(8,128)S(1)}, u32[]{:S(2)}, u32[]{:S(2)}) collective-permute-start(f32[256,256]{0,1:T(8,128)S(1)} %get-tuple-element.12), channel_id=1, source_target_pairs={{0,8},{8,0},{16,24},{24,16},{32,40},{40,32},{48,56},{56,48},{64,72... | collective-permute-start | bytes 786440 | tf_op jit(solution)/shard_map/ppermute | solution.py:24
  104.8 32.9 %collective-permute-start.3 = (f32[256,1024]{1,0:T(8,128)S(1)}, f32[256,1024]{1,0:T(8,128)S(1)}, u32[]{:S(2)}, u32[]{:S(2)}) collective-permute-start(f32[256,1024]{1,0:T(8,128)S(1)} %subtract_select_fusion.5), channel_id=1, source_target_pairs={{0,16},{8,24},{16,0},{24,8},{32,48},{40,56},{48,32},{56,40},{64,80... | collective-permute-start | bytes 3145736 | tf_op jit(solution)/shard_map/ppermute | solution.py:24
  108.3 29.4 %collective-permute-start.2 = (f32[256,256]{0,1:T(8,128)S(1)}, f32[256,256]{0,1:T(8,128)S(1)}, u32[]{:S(2)}, u32[]{:S(2)}) collective-permute-start(f32[256,256]{0,1:T(8,128)S(1)} %get-tuple-element.11), channel_id=1, source_target_pairs={{0,16},{8,24},{16,0},{24,8},{32,48},{40,56},{48,32},{56,40},{64,80... | collective-permute-start | bytes 786440 | tf_op jit(solution)/shard_map/ppermute | solution.py:24
  141.2 61.2 %collective-permute-start.5 = (f32[256,1024]{1,0:T(8,128)S(1)}, f32[256,1024]{1,0:T(8,128)S(1)}, u32[]{:S(2)}, u32[]{:S(2)}) collective-permute-start(f32[256,1024]{1,0:T(8,128)S(1)} %subtract_select_fusion.4), channel_id=1, source_target_pairs={{0,32},{8,40},{16,48},{24,56},{32,0},{40,8},{48,16},{56,24},{64,96... | collective-permute-start | bytes 3145736 | tf_op jit(solution)/shard_map/ppermute | solution.py:24
  145.8 56.5 %collective-permute-start.4 = (f32[256,256]{0,1:T(8,128)S(1)}, f32[256,256]{0,1:T(8,128)S(1)}, u32[]{:S(2)}, u32[]{:S(2)}) collective-permute-start(f32[256,256]{0,1:T(8,128)S(1)} %get-tuple-element.10), channel_id=1, source_target_pairs={{0,32},{8,40},{16,48},{24,56},{32,0},{40,8},{48,16},{56,24},{64,96... | collective-permute-start | bytes 786440 | tf_op jit(solution)/shard_map/ppermute | solution.py:24
  205.8 65.2 %collective-permute-start.7 = (f32[256,1024]{1,0:T(8,128)S(1)}, f32[256,1024]{1,0:T(8,128)S(1)}, u32[]{:S(2)}, u32[]{:S(2)}) collective-permute-start(f32[256,1024]{1,0:T(8,128)S(1)} %subtract_select_fusion.3), channel_id=1, source_target_pairs={{0,64},{8,72},{16,80},{24,88},{32,96},{40,104},{48,112},{56,120},{... | collective-permute-start | bytes 3145736 | tf_op jit(solution)/shard_map/ppermute | solution.py:24
  213.7 57.3 %collective-permute-start.6 = (f32[256,256]{0,1:T(8,128)S(1)}, f32[256,256]{0,1:T(8,128)S(1)}, u32[]{:S(2)}, u32[]{:S(2)}) collective-permute-start(f32[256,256]{0,1:T(8,128)S(1)} %get-tuple-element.9), channel_id=1, source_target_pairs={{0,64},{8,72},{16,80},{24,88},{32,96},{40,104},{48,112},{56,120},{... | collective-permute-start | bytes 786440 | tf_op jit(solution)/shard_map/ppermute | solution.py:24
  274.5 31.8 %collective-permute-start.9 = (f32[256,1024]{1,0:T(8,128)S(1)}, f32[256,1024]{1,0:T(8,128)S(1)}, u32[]{:S(2)}, u32[]{:S(2)}) collective-permute-start(f32[256,1024]{1,0:T(8,128)S(1)} %subtract_select_fusion.2), channel_id=1, source_target_pairs={{0,128},{8,136},{16,144},{24,152},{32,160},{40,168},{48,176},{56,1... | collective-permute-start | bytes 3145736 | tf_op jit(solution)/shard_map/ppermute | solution.py:24
  276.9 29.3 %collective-permute-start.8 = (f32[256,256]{0,1:T(8,128)S(1)}, f32[256,256]{0,1:T(8,128)S(1)}, u32[]{:S(2)}, u32[]{:S(2)}) collective-permute-start(f32[256,256]{0,1:T(8,128)S(1)} %get-tuple-element.8), channel_id=1, source_target_pairs={{0,128},{8,136},{16,144},{24,152},{32,160},{40,168},{48,176},{56,1... | collective-permute-start | bytes 786440 | tf_op jit(solution)/shard_map/ppermute | solution.py:24
  309.7 32.4 %collective-permute-start.11 = (f32[256,1024]{1,0:T(8,128)S(1)}, f32[256,1024]{1,0:T(8,128)S(1)}, u32[]{:S(2)}, u32[]{:S(2)}) collective-permute-start(f32[256,1024]{1,0:T(8,128)S(1)} %subtract_select_fusion.1), channel_id=1, source_target_pairs={{0,256},{8,264},{16,272},{24,280},{32,288},{40,296},{48,304},{56,3... | collective-permute-start | bytes 3145736 | tf_op jit(solution)/shard_map/ppermute | solution.py:24
  313.7 28.4 %collective-permute-start.10 = (f32[256,256]{0,1:T(8,128)S(1)}, f32[256,256]{0,1:T(8,128)S(1)}, u32[]{:S(2)}, u32[]{:S(2)}) collective-permute-start(f32[256,256]{0,1:T(8,128)S(1)} %get-tuple-element.7), channel_id=1, source_target_pairs={{0,256},{8,264},{16,272},{24,280},{32,288},{40,296},{48,304},{56,3... | collective-permute-start | bytes 786440 | tf_op jit(solution)/shard_map/ppermute | solution.py:24
Sparse Core Ops, SparseCore 0:
  10.4 59.2 all-gather.1
where the time goes:
time: 355 us; the launch traced here: 354 us
  waiting for transfers between devices  248 us (70%)
  starting transfers between devices  40.5 us (11%)
  matrix products  28.9 us (8%)
  local copies, waits for them, and re-layouts  17.5 us (5%)
  between operations  13.8 us (4%)
  other arithmetic  5.28 us (1%)
    ppermute x12, waiting for transfers between devices, swapped(): return lax.ppermute(value, axis, pairs)  189 us
    all_gather x1, waiting for transfers between devices, turned_gather(): whole, at, done = (lax.all_gather(both, axis, axis=0, tiled=True), 0, [])  59.3 us
    ppermute x12, starting transfers between devices, swapped(): return lax.ppermute(value, axis, pairs)  40.5 us
    slice x3, local copies, waits for them, and re-layouts, turned_gather(): section = whole[:, at:at + t[0].size].reshape(-1, *t.shape[1:])  8.18 us
    dot_general x6, matrix products, combine(): jnp.einsum('kb,kc->bc', chosen_y, follower_rows, precision=highest)  7.63 us
    dot_general x6, matrix products, combine(): jnp.einsum('bk,kc->bc', chosen_y, coupling, precision=highest)  7.1 us
  transfers between devices with their start and end apart: 13, of which 7 were waited for; matrix products, arithmetic and copies ran while one was open for 5% of the time, Pallas kernels for 0%

commit v1 on v0

--- a/solution.py
+++ b/solution.py
@@ -10,7 +10,13 @@
 def turned_gather(arrays, axis, dims):
     turned = [jnp.moveaxis(a, dim, 0) for a, dim in zip(arrays, dims)]
     both = jnp.concatenate([t.reshape(len(t), -1) for t in turned], axis=1)
-    whole, at, done = (lax.all_gather(both, axis, axis=0, tiled=True), 0, [])
+    whole, at, done = (
+        jnp.concatenate(
+            lax.all_to_all(jnp.stack([both] * lax.axis_size(axis)), axis, 0, 0), axis=0
+        ),
+        0,
+        [],
+    )
     for t, dim in zip(turned, dims):
         section = whole[:, at : at + t[0].size].reshape(-1, *t.shape[1:])
         done.append(jnp.moveaxis(section, 0, dim))

time: 355 us -> 384 us (1.082)
  the two profiles are of different devices: /device:TPU:2 before, /device:TPU:198 now
where the time goes in v1:
time: 384 us
  waiting for transfers between devices  280 us (73%)
  starting transfers between devices  48 us (12%)
  matrix products  29.8 us (8%)
  local copies, waits for them, and re-layouts  21.1 us (5%)
  other arithmetic  4.5 us (1%)
    ppermute x12, waiting for transfers between devices, swapped(): return lax.ppermute(value, axis, pairs)  189 us
    all_to_all x1, waiting for transfers between devices, turned_gather(): lax.all_to_all(jnp.stack([both] * lax.axis_size(axis)), axis, 0, 0)  90.8 us
    ppermute x12, starting transfers between devices, swapped(): return lax.ppermute(value, axis, pairs)  40.7 us
    slice x3, local copies, waits for them, and re-layouts, turned_gather(): section = whole[:, at:at + t[0].size].reshape(-1, *t.shape[1:])  9.83 us
  transfers between devices with their start and end apart: 13, of which 7 were waited for; matrix products, arithmetic and copies ran while one was open for 5% of the time, Pallas kernels for 0%

profile of v1, /device:TPU:198, one launch (start us, length us, event | category | flops | bytes accessed | tf_op | source)
XLA Modules:
  0.0 383.6 jit_solution(6422449871551888724)
XLA Ops:
  0.0 0.9 copy.17
  0.9 0.9 copy.18
  1.9 0.9 pad_maximum_fusion.1
  2.8 2.2 stack.2
  5.0 7.2 %all-to-all-start = ((f32[8,32,3840]{2,1,0:T(8,128)}), f32[8,32,3840]{2,1,0:T(8,128)}, u32[]{:S(2)}, u32[]{:S(2)}) async-start(f32[8,32,3840]{2,1,0:T(8,128)} %stack.2), calls=%async_computation | async-start | bytes 7864320 | tf_op jit(solution)/shard_map/all_to_all | solution.py:15
  12.2 90.8 %all-to-all-done = f32[8,32,3840]{2,1,0:T(8,128)} async-done(((f32[8,32,3840]{2,1,0:T(8,128)}), f32[8,32,3840]{2,1,0:T(8,128)}, u32[]{:S(2)}, u32[]{:S(2)}) %all-to-all-start) | async-done | bytes 3932192 | tf_op jit(solution)/shard_map/all_to_all | solution.py:15
  103.0 0.0 copy-done.2
  103.0 2.9 fusion.43
  105.9 0.0 copy-start.3
  105.9 2.1 fusion.45
  108.1 0.0 copy-done.3
  108.1 3.0 convolution_subtract_fusion
  111.1 1.2 fusion.140
  112.2 1.9 collective-permute-start.1
  114.1 3.8 fusion.139
  117.9 3.0 copy.15
  121.0 3.1 copy.16
  124.0 3.0 copy.13
  127.0 3.0 copy.14
  130.0 2.1 fusion.70
  132.2 0.0 copy-start.1
  132.2 2.5 collective-permute-start
  134.7 1.1 collective-permute-done
  135.9 0.0 collective-permute-done.1
  135.9 0.0 copy-done
  135.9 2.3 fusion.27
  138.2 1.2 fusion.25
  139.4 1.2 subtract_select_fusion.5
  140.5 1.9 collective-permute-start.3
  142.5 4.1 %collective-permute-start.2 = (f32[256,256]{0,1:T(8,128)S(1)}, f32[256,256]{0,1:T(8,128)S(1)}, u32[]{:S(2)}, u32[]{:S(2)}) collective-permute-start(f32[256,256]{0,1:T(8,128)S(1)} %get-tuple-element.11), channel_id=1, source_target_pairs={{0,16},{8,24},{16,0},{24,8},{32,48},{40,56},{48,32},{56,40},{64,80... | collective-permute-start | bytes 786440 | tf_op jit(solution)/shard_map/ppermute | solution.py:30
  146.6 26.9 %collective-permute-done.2 = f32[256,256]{0,1:T(8,128)S(1)} collective-permute-done((f32[256,256]{0,1:T(8,128)S(1)}, f32[256,256]{0,1:T(8,128)S(1)}, u32[]{:S(2)}, u32[]{:S(2)}) %collective-permute-start.2) | collective-permute-done | bytes 262176 | tf_op jit(solution)/shard_map/ppermute | solution.py:30
  173.5 0.0 collective-permute-done.3
  173.5 1.1 fusion.22
  174.6 1.2 fusion.20
  175.8 1.2 subtract_select_fusion.4
  176.9 1.9 collective-permute-start.5
  178.9 4.8 %collective-permute-start.4 = (f32[256,256]{0,1:T(8,128)S(1)}, f32[256,256]{0,1:T(8,128)S(1)}, u32[]{:S(2)}, u32[]{:S(2)}) collective-permute-start(f32[256,256]{0,1:T(8,128)S(1)} %get-tuple-element.10), channel_id=1, source_target_pairs={{0,32},{8,40},{16,48},{24,56},{32,0},{40,8},{48,16},{56,24},{64,96... | collective-permute-start | bytes 786440 | tf_op jit(solution)/shard_map/ppermute | solution.py:30
  183.7 54.3 %collective-permute-done.4 = f32[256,256]{0,1:T(8,128)S(1)} collective-permute-done((f32[256,256]{0,1:T(8,128)S(1)}, f32[256,256]{0,1:T(8,128)S(1)}, u32[]{:S(2)}, u32[]{:S(2)}) %collective-permute-start.4) | collective-permute-done | bytes 262176 | tf_op jit(solution)/shard_map/ppermute | solution.py:30
  238.0 0.0 collective-permute-done.5
  238.0 1.1 fusion.17
  239.1 1.2 fusion.15
  240.3 1.2 subtract_select_fusion.3
  241.5 8.2 %collective-permute-start.7 = (f32[256,1024]{1,0:T(8,128)S(1)}, f32[256,1024]{1,0:T(8,128)S(1)}, u32[]{:S(2)}, u32[]{:S(2)}) collective-permute-start(f32[256,1024]{1,0:T(8,128)S(1)} %subtract_select_fusion.3), channel_id=1, source_target_pairs={{0,64},{8,72},{16,80},{24,88},{32,96},{40,104},{48,112},{56,120},{... | collective-permute-start | bytes 3145736 | tf_op jit(solution)/shard_map/ppermute | solution.py:30
  249.7 1.9 collective-permute-start.6
  251.6 55.6 %collective-permute-done.6 = f32[256,256]{0,1:T(8,128)S(1)} collective-permute-done((f32[256,256]{0,1:T(8,128)S(1)}, f32[256,256]{0,1:T(8,128)S(1)}, u32[]{:S(2)}, u32[]{:S(2)}) %collective-permute-start.6) | collective-permute-done | bytes 262176 | tf_op jit(solution)/shard_map/ppermute | solution.py:30
  307.2 0.0 collective-permute-done.7
  307.2 1.1 fusion.12
  308.3 1.2 fusion.10
  309.5 1.2 subtract_select_fusion.2
  310.6 2.7 collective-permute-start.9
  313.3 3.4 collective-permute-start.8
  316.7 25.9 %collective-permute-done.8 = f32[256,256]{0,1:T(8,128)S(1)} collective-permute-done((f32[256,256]{0,1:T(8,128)S(1)}, f32[256,256]{0,1:T(8,128)S(1)}, u32[]{:S(2)}, u32[]{:S(2)}) %collective-permute-start.8) | collective-permute-done | bytes 262176 | tf_op jit(solution)/shard_map/ppermute | solution.py:30
  342.6 0.0 collective-permute-done.9
  342.6 1.1 fusion.7
  343.7 1.2 fusion.5
  344.9 1.2 subtract_select_fusion.1
  346.0 3.3 collective-permute-start.11
  349.4 4.0 %collective-permute-start.10 = (f32[256,256]{0,1:T(8,128)S(1)}, f32[256,256]{0,1:T(8,128)S(1)}, u32[]{:S(2)}, u32[]{:S(2)}) collective-permute-start(f32[256,256]{0,1:T(8,128)S(1)} %get-tuple-element.7), channel_id=1, source_target_pairs={{0,256},{8,264},{16,272},{24,280},{32,288},{40,296},{48,304},{56,3... | collective-permute-start | bytes 786440 | tf_op jit(solution)/shard_map/ppermute | solution.py:30
  353.4 25.2 %collective-permute-done.10 = f32[256,256]{0,1:T(8,128)S(1)} collective-permute-done((f32[256,256]{0,1:T(8,128)S(1)}, f32[256,256]{0,1:T(8,128)S(1)}, u32[]{:S(2)}, u32[]{:S(2)}) %collective-permute-start.10) | collective-permute-done | bytes 262176 | tf_op jit(solution)/shard_map/ppermute | solution.py:30
  378.6 0.0 collective-permute-done.11
  378.7 1.1 fusion.2
  379.7 1.2 fusion
  380.9 1.2 subtract_select_fusion
  382.1 1.5 pad_maximum_fusion
  (4 shorter events, 0.0 us)
Async XLA Ops:
  5.0 98.0 %copy-start.2 = (f32[512,1024]{1,0:T(8,128)S(1)}, f32[512,1024]{1,0:T(8,128)}, u32[]{:S(2)}) copy-start(f32[512,1024]{1,0:T(8,128)} %param.5) | copy-start | bytes 6291460
  5.0 98.0 %all-to-all-start = ((f32[8,32,3840]{2,1,0:T(8,128)}), f32[8,32,3840]{2,1,0:T(8,128)}, u32[]{:S(2)}, u32[]{:S(2)}) async-start(f32[8,32,3840]{2,1,0:T(8,128)} %stack.2), calls=%async_computation | async-start | bytes 7864320 | tf_op jit(solution)/shard_map/all_to_all | solution.py:15
  105.9 2.2 copy-start.3
  112.2 23.7 %collective-permute-start.1 = (f32[256,1024]{1,0:T(8,128)}, f32[256,1024]{1,0:T(8,128)}, u32[]{:S(2)}, u32[]{:S(2)}) collective-permute-start(f32[256,1024]{1,0:T(8,128)} %get-tuple-element.13), channel_id=1, source_target_pairs={{0,8},{8,0},{16,24},{24,16},{32,40},{40,32},{48,56},{56,48},{64,72... | collective-permute-start | bytes 3145736 | tf_op jit(solution)/shard_map/ppermute | solution.py:30
  130.0 5.8 %copy-start = (f32[256,6,256]{2,0,1:T(8,128)S(1)}, f32[256,6,256]{2,0,1:T(8,128)}, u32[]{:S(2)}) copy-start(f32[256,6,256]{2,0,1:T(8,128)} %copy.16) | copy-start | bytes 4718596
  132.2 6.0 %copy-start.1 = (f32[256,6,256]{2,0,1:T(8,128)S(1)}, f32[256,6,256]{2,0,1:T(8,128)}, u32[]{:S(2)}) copy-start(f32[256,6,256]{2,0,1:T(8,128)} %copy.14) | copy-start | bytes 4718596
  132.2 3.7 collective-permute-start
  140.5 33.0 %collective-permute-start.3 = (f32[256,1024]{1,0:T(8,128)S(1)}, f32[256,1024]{1,0:T(8,128)S(1)}, u32[]{:S(2)}, u32[]{:S(2)}) collective-permute-start(f32[256,1024]{1,0:T(8,128)S(1)} %subtract_select_fusion.5), channel_id=1, source_target_pairs={{0,16},{8,24},{16,0},{24,8},{32,48},{40,56},{48,32},{56,40},{64,80... | collective-permute-start | bytes 3145736 | tf_op jit(solution)/shard_map/ppermute | solution.py:30
  142.5 31.0 %collective-permute-start.2 = (f32[256,256]{0,1:T(8,128)S(1)}, f32[256,256]{0,1:T(8,128)S(1)}, u32[]{:S(2)}, u32[]{:S(2)}) collective-permute-start(f32[256,256]{0,1:T(8,128)S(1)} %get-tuple-element.11), channel_id=1, source_target_pairs={{0,16},{8,24},{16,0},{24,8},{32,48},{40,56},{48,32},{56,40},{64,80... | collective-permute-start | bytes 786440 | tf_op jit(solution)/shard_map/ppermute | solution.py:30
  176.9 61.1 %collective-permute-start.5 = (f32[256,1024]{1,0:T(8,128)S(1)}, f32[256,1024]{1,0:T(8,128)S(1)}, u32[]{:S(2)}, u32[]{:S(2)}) collective-permute-start(f32[256,1024]{1,0:T(8,128)S(1)} %subtract_select_fusion.4), channel_id=1, source_target_pairs={{0,32},{8,40},{16,48},{24,56},{32,0},{40,8},{48,16},{56,24},{64,96... | collective-permute-start | bytes 3145736 | tf_op jit(solution)/shard_map/ppermute | solution.py:30
  178.9 59.2 %collective-permute-start.4 = (f32[256,256]{0,1:T(8,128)S(1)}, f32[256,256]{0,1:T(8,128)S(1)}, u32[]{:S(2)}, u32[]{:S(2)}) collective-permute-start(f32[256,256]{0,1:T(8,128)S(1)} %get-tuple-element.10), channel_id=1, source_target_pairs={{0,32},{8,40},{16,48},{24,56},{32,0},{40,8},{48,16},{56,24},{64,96... | collective-permute-start | bytes 786440 | tf_op jit(solution)/shard_map/ppermute | solution.py:30
  241.5 65.7 %collective-permute-start.7 = (f32[256,1024]{1,0:T(8,128)S(1)}, f32[256,1024]{1,0:T(8,128)S(1)}, u32[]{:S(2)}, u32[]{:S(2)}) collective-permute-start(f32[256,1024]{1,0:T(8,128)S(1)} %subtract_select_fusion.3), channel_id=1, source_target_pairs={{0,64},{8,72},{16,80},{24,88},{32,96},{40,104},{48,112},{56,120},{... | collective-permute-start | bytes 3145736 | tf_op jit(solution)/shard_map/ppermute | solution.py:30
  249.7 57.5 %collective-permute-start.6 = (f32[256,256]{0,1:T(8,128)S(1)}, f32[256,256]{0,1:T(8,128)S(1)}, u32[]{:S(2)}, u32[]{:S(2)}) collective-permute-start(f32[256,256]{0,1:T(8,128)S(1)} %get-tuple-element.9), channel_id=1, source_target_pairs={{0,64},{8,72},{16,80},{24,88},{32,96},{40,104},{48,112},{56,120},{... | collective-permute-start | bytes 786440 | tf_op jit(solution)/shard_map/ppermute | solution.py:30
  310.6 32.0 %collective-permute-start.9 = (f32[256,1024]{1,0:T(8,128)S(1)}, f32[256,1024]{1,0:T(8,128)S(1)}, u32[]{:S(2)}, u32[]{:S(2)}) collective-permute-start(f32[256,1024]{1,0:T(8,128)S(1)} %subtract_select_fusion.2), channel_id=1, source_target_pairs={{0,128},{8,136},{16,144},{24,152},{32,160},{40,168},{48,176},{56,1... | collective-permute-start | bytes 3145736 | tf_op jit(solution)/shard_map/ppermute | solution.py:30
  313.3 29.3 %collective-permute-start.8 = (f32[256,256]{0,1:T(8,128)S(1)}, f32[256,256]{0,1:T(8,128)S(1)}, u32[]{:S(2)}, u32[]{:S(2)}) collective-permute-start(f32[256,256]{0,1:T(8,128)S(1)} %get-tuple-element.8), channel_id=1, source_target_pairs={{0,128},{8,136},{16,144},{24,152},{32,160},{40,168},{48,176},{56,1... | collective-permute-start | bytes 786440 | tf_op jit(solution)/shard_map/ppermute | solution.py:30
  346.0 32.6 %collective-permute-start.11 = (f32[256,1024]{1,0:T(8,128)S(1)}, f32[256,1024]{1,0:T(8,128)S(1)}, u32[]{:S(2)}, u32[]{:S(2)}) collective-permute-start(f32[256,1024]{1,0:T(8,128)S(1)} %subtract_select_fusion.1), channel_id=1, source_target_pairs={{0,256},{8,264},{16,272},{24,280},{32,288},{40,296},{48,304},{56,3... | collective-permute-start | bytes 3145736 | tf_op jit(solution)/shard_map/ppermute | solution.py:30
  349.4 29.3 %collective-permute-start.10 = (f32[256,256]{0,1:T(8,128)S(1)}, f32[256,256]{0,1:T(8,128)S(1)}, u32[]{:S(2)}, u32[]{:S(2)}) collective-permute-start(f32[256,256]{0,1:T(8,128)S(1)} %get-tuple-element.7), channel_id=1, source_target_pairs={{0,256},{8,264},{16,272},{24,280},{32,288},{40,296},{48,304},{56,3... | collective-permute-start | bytes 786440 | tf_op jit(solution)/shard_map/ppermute | solution.py:30
